TPU v7x, 128 devices: a whole 4x4x4 slice. The times are simulated.
128 devices in a mesh: seq: 16 (over z_lo, x, core), res: 8 (over y, z_hi).
Axes of the slice: x: 4, y: 4, z: 4 (z_hi: 2, z_lo: 2; z = z_hi * 2 + z_lo), core: 2. Of those that a mesh axis runs over, the one named last changes fastest.
Arguments:
- states: bfloat16 [512, 256, 768], P('seq', 'res'), may hold values from -6 to 6
- row_query: bfloat16 [768, 768], replicated, as said below
- row_key: bfloat16 [768, 768], replicated
- row_value: bfloat16 [768, 768], replicated, may hold values from -0.21875 to 0.21875
- row_out: bfloat16 [768, 768], replicated, may hold values from -0.21875 to 0.21875
- col_query: bfloat16 [768, 768], replicated, as said below
- col_key: bfloat16 [768, 768], replicated
- col_value: bfloat16 [768, 768], replicated, may hold values from -0.21875 to 0.21875
- col_out: bfloat16 [768, 768], replicated, may hold values from -0.21875 to 0.21875
Outputs:
- updated: bfloat16 [512, 256, 768], P('seq', 'res')
Inputs may be any that keep to these rules, and one draw needn't show every extreme that they name: No bound on the size of row_query and row_key entries or of the scores they give is promised. No bound on the size of col_query and col_key entries or of the scores they give is promised.
All inputs are finite; a program needn't handle non-finite values.
Results may differ from a plain program's by a relative error of at most 0.02.
Values may be sent and summed in bfloat16 or wider, within the bound.
A program may use at most 128 MiB of HBM per device.

v0:
```python
import math
import jax
import jax.numpy as jnp
from jax import lax
from jax.sharding import PartitionSpec as P

D = 768
HEADS = 12


def normalize(states):
    values = states.astype(jnp.float32)
    center = values - jnp.mean(values, axis=-1, keepdims=True)
    spread = jnp.mean(center * center, axis=-1, keepdims=True)
    return (center * lax.rsqrt(spread + 1e-05)).astype(jnp.bfloat16)


def project(inputs, weight):
    return jnp.dot(inputs, weight, preferred_element_type=jnp.float32)


def split_heads(field):
    return field.reshape(field.shape[0], field.shape[1], HEADS, D // HEADS)


def on_device(
    states, row_query, row_key, row_value, row_out, col_query, col_key, col_value, col_out
):
    row_count, col_count = (states.shape[0], states.shape[1])
    head_dim = D // HEADS
    all_rows = row_count * lax.axis_size("seq")
    tied_scale = head_dim ** (-0.5) / math.sqrt(all_rows)
    normed = normalize(states)
    q1 = project(normed, row_query).astype(jnp.bfloat16)
    k1 = project(normed, row_key).astype(jnp.bfloat16)
    v1 = project(normed, row_value).astype(jnp.bfloat16)
    q_moved, k_moved, v_moved = (
        lax.all_to_all(q1, "res", split_axis=0, concat_axis=1, tiled=True),
        lax.all_to_all(k1, "res", split_axis=0, concat_axis=1, tiled=True),
        lax.all_to_all(v1, "res", split_axis=0, concat_axis=1, tiled=True),
    )
    partial_value = (
        jnp.einsum(
            "rihd,rjhd->hij",
            split_heads(q_moved),
            split_heads(k_moved),
            preferred_element_type=jnp.float32,
        )
        * tied_scale
    )
    tied = lax.psum(partial_value, ("seq", "res"))
    prob1 = jax.nn.softmax(tied, axis=-1).astype(jnp.bfloat16)
    o_moved = jnp.einsum(
        "hij,rjhd->rihd", prob1, split_heads(v_moved), preferred_element_type=jnp.float32
    ).astype(jnp.bfloat16)
    o_moved = o_moved.reshape(o_moved.shape[0], o_moved.shape[1], D)
    o1 = lax.all_to_all(o_moved, "res", split_axis=1, concat_axis=0, tiled=True)
    mid = (states.astype(jnp.float32) + project(o1, row_out)).astype(jnp.bfloat16)
    normed2 = normalize(mid)
    q2 = project(normed2, col_query).astype(jnp.bfloat16)
    k2 = project(normed2, col_key).astype(jnp.bfloat16)
    v2 = project(normed2, col_value).astype(jnp.bfloat16)
    q_cols, k_cols, v_cols = (
        lax.all_to_all(q2, "seq", split_axis=1, concat_axis=0, tiled=True),
        lax.all_to_all(k2, "seq", split_axis=1, concat_axis=0, tiled=True),
        lax.all_to_all(v2, "seq", split_axis=1, concat_axis=0, tiled=True),
    )
    gathered_rows, local_cols = (q_cols.shape[0], q_cols.shape[1])

    def arrange(field):
        return field.reshape(gathered_rows, local_cols, HEADS, head_dim).transpose(1, 0, 2, 3)

    def attend(triple):
        query_col, key_col, value_col = triple
        score = jnp.einsum(
            "rhd,shd->hrs", query_col, key_col, preferred_element_type=jnp.float32
        ) * head_dim ** (-0.5)
        prob2 = jax.nn.softmax(score, axis=-1).astype(jnp.bfloat16)
        return jnp.einsum(
            "hrs,shd->rhd", prob2, value_col, preferred_element_type=jnp.float32
        ).astype(jnp.bfloat16)

    o2 = lax.map(attend, (arrange(q_cols), arrange(k_cols), arrange(v_cols)))
    o2 = o2.reshape(local_cols, gathered_rows, D).transpose(1, 0, 2)
    colupd = project(o2, col_out).astype(jnp.bfloat16)
    colupd = lax.all_to_all(colupd, "seq", split_axis=0, concat_axis=1, tiled=True)
    return (mid.astype(jnp.float32) + colupd.astype(jnp.float32)).astype(jnp.bfloat16)


def solution(mesh):
    placed = (P("seq", "res", None), P(), P(), P(), P(), P(), P(), P(), P())
    return jax.shard_map(
        on_device, mesh=mesh, in_specs=placed, out_specs=P("seq", "res", None), check_vma=False
    )
```

profile of v0, /device:TPU:1, one launch (start us, length us, event | category | flops | bytes accessed | tf_op | source)
XLA Modules:
  0.0 487.7 jit_solution(7350773890253013936)
XLA Ops:
  11.7 8.3 %all-to-all-start.1 = ((bf16[32,32,768]{2,1,0:T(8,128)(2,1)}), bf16[32,32,768]{2,1,0:T(8,128)(2,1)}, u32[]{:S(2)}, u32[]{:S(2)}) async-start(bf16[32,32,768]{2,1,0:T(8,128)(2,1)} %convolution_convert_fusion.5), calls=%async_computation.1 | async-start | bytes 3145728 | tf_op jit(solution)/shard_map/all_to_all | solution.py:38
  20.1 3.9 convolution_convert_fusion.4
  23.9 19.3 %all-to-all-done.1 = bf16[32,32,768]{2,1,0:T(8,128)(2,1)} async-done(((bf16[32,32,768]{2,1,0:T(8,128)(2,1)}), bf16[32,32,768]{2,1,0:T(8,128)(2,1)}, u32[]{:S(2)}, u32[]{:S(2)}) %all-to-all-start.1) | async-done | bytes 1572896 | tf_op jit(solution)/shard_map/all_to_all | solution.py:38
  43.2 4.3 all-to-all-start.2
  50.3 5.9 %reshape.63 = bf16[4,256,12,64]{3,2,1,0:T(8,128)(2,1)} reshape(bf16[4,8,32,768]{3,2,1,0:T(8,128)(2,1)} %bitcast.147) | data formatting | bytes 3145728 | tf_op jit(solution)/shard_map/reshape | solution.py:23
  56.2 13.5 %all-to-all-done.2 = bf16[32,32,768]{2,1,0:T(8,128)(2,1)} async-done(((bf16[32,32,768]{2,1,0:T(8,128)(2,1)}), bf16[32,32,768]{2,1,0:T(8,128)(2,1)}, u32[]{:S(2)}, u32[]{:S(2)}) %all-to-all-start.2) | async-done | bytes 1572896 | tf_op jit(solution)/shard_map/all_to_all | solution.py:39
  72.3 5.9 %reshape.64 = bf16[4,256,12,64]{3,2,1,0:T(8,128)(2,1)} reshape(bf16[4,8,32,768]{3,2,1,0:T(8,128)(2,1)} %bitcast.148) | data formatting | bytes 3145728 | tf_op jit(solution)/shard_map/reshape | solution.py:23
  78.2 6.7 %bitcast_multiply_fusion = f32[12,256,256]{2,1,0:T(8,128)} fusion(bf16[4,256,12,64]{3,2,1,0:T(8,128)(2,1)} %reshape.64, bf16[4,256,12,64]{3,2,1,0:T(8,128)(2,1)} %reshape.63), kind=kOutput, calls=%fused_computation.43 | convolution fusion | flops 403439616 | bytes 6291456 | tf_op jit(solution)/shard_map/rihd,rjhd->hij/dot_general | solution.py:43
  87.7 26.8 %all_to_all.117 = bf16[32,32,768]{2,1,0:T(8,128)(2,1)S(1)} all-to-all(bf16[32,32,768]{2,1,0:T(8,128)(2,1)S(1)} %convolution_convert_fusion.6), channel_id=1, replica_groups=mesh['seq'=16,'res'=8] {'res'}, dimensions={0} | all-to-all | bytes 3145728 | tf_op jit(solution)/shard_map/all_to_all | solution.py:40
  115.8 5.9 %reshape.62 = bf16[4,256,12,64]{3,2,1,0:T(8,128)(2,1)} reshape(bf16[4,8,32,768]{3,2,1,0:T(8,128)(2,1)} %bitcast.149) | data formatting | bytes 3145728 | tf_op jit(solution)/shard_map/reshape | solution.py:23
  121.7 123.8 %all-reduce.2.cloned.1.call-done = f32[12,256,256]{2,1,0:T(8,128)} async-done(((f32[12,256,256]{2,1,0:T(8,128)}), f32[12,256,256]{2,1,0:T(8,128)}) %all-reduce.2.cloned.1.call-update) | async-done | bytes 3145744 | tf_op jit(solution)/shard_map/psum | solution.py:51
  245.5 3.8 fusion.92
  249.3 12.5 %fusion.63 = bf16[4,256,12,64]{1,3,0,2:T(8,128)(2,1)} fusion(f32[12,256]{1,0:T(8,128)S(1)} %fusion.92, bf16[4,256,12,64]{3,2,1,0:T(8,128)(2,1)} %reshape.62, f32[12,256,256]{2,1,0:T(8,128)} %all-reduce.2.cloned.1.call-done), kind=kOutput, calls=%fused_computation.68 | convolution fusion | flops 405802240 | bytes 6303744 | tf_op jit(solution)/shard_map/hij,rjhd->rihd/dot_general | solution.py:53
  268.2 25.9 %all_to_all.118 = bf16[4,256,768]{2,0,1:T(4,128)(2,1)S(1)} all-to-all(bf16[4,256,768]{2,0,1:T(4,128)(2,1)} %copy.42), channel_id=1, replica_groups=mesh['seq'=16,'res'=8] {'res'}, dimensions={1} | all-to-all | bytes 3145728 | tf_op jit(solution)/shard_map/all_to_all | solution.py:57
  301.3 6.3 %all-to-all-start.6 = ((bf16[32,32,768]{2,0,1:T(8,128)(2,1)}), bf16[32,32,768]{2,0,1:T(8,128)(2,1)S(1)}, u32[]{:S(2)}, u32[]{:S(2)}) async-start(bf16[32,32,768]{2,0,1:T(8,128)(2,1)} %copy.49), calls=%async_computation.6 | async-start | bytes 3145728 | tf_op jit(solution)/shard_map/all_to_all | solution.py:65
  312.9 16.3 %all-to-all-done.6 = bf16[32,32,768]{2,0,1:T(8,128)(2,1)S(1)} async-done(((bf16[32,32,768]{2,0,1:T(8,128)(2,1)}), bf16[32,32,768]{2,0,1:T(8,128)(2,1)S(1)}, u32[]{:S(2)}, u32[]{:S(2)}) %all-to-all-start.6) | async-done | bytes 1572896 | tf_op jit(solution)/shard_map/all_to_all | solution.py:65
  329.1 4.9 all-to-all-start.5
  339.3 16.4 %all-to-all-done.5 = bf16[32,32,768]{2,0,1:T(8,128)(2,1)} async-done(((bf16[32,32,768]{2,0,1:T(8,128)(2,1)}), bf16[32,32,768]{2,0,1:T(8,128)(2,1)}, u32[]{:S(2)}, u32[]{:S(2)}) %all-to-all-start.5) | async-done | bytes 1572896 | tf_op jit(solution)/shard_map/all_to_all | solution.py:64
  355.7 13.4 %all-to-all-start.4 = ((bf16[32,32,768]{2,0,1:T(8,128)(2,1)}), bf16[32,32,768]{2,0,1:T(8,128)(2,1)}, u32[]{:S(2)}, u32[]{:S(2)}) async-start(bf16[32,32,768]{2,0,1:T(8,128)(2,1)} %copy.45), calls=%async_computation.4 | async-start | bytes 3145728 | tf_op jit(solution)/shard_map/all_to_all | solution.py:66
  370.4 5.9 %reshape.68 = bf16[512,2,12,64]{3,2,0,1:T(8,128)(2,1)} reshape(bf16[16,32,2,768]{3,1,0,2:T(8,128)(2,1)} %bitcast.150) | data formatting | bytes 3145728 | tf_op jit(solution)/shard_map/reshape | solution.py:71
  376.3 5.3 %copy.53 = bf16[2,512,12,64]{1,3,2,0:T(8,128)(2,1)} copy(bf16[2,512,12,64]{3,2,1,0:T(8,128)(2,1)} %bitcast.140) | data formatting | bytes 3145728 | tf_op jit(solution)/shard_map/while | solution.py:83
  383.2 3.9 reshape.67
  387.0 5.3 %copy.52 = bf16[2,512,12,64]{1,3,2,0:T(8,128)(2,1)} copy(bf16[2,512,12,64]{3,2,1,0:T(8,128)(2,1)} %bitcast.141) | data formatting | bytes 3145728 | tf_op jit(solution)/shard_map/while | solution.py:83
  393.9 3.9 reshape.66
  397.8 5.5 %copy.51 = bf16[2,512,12,64]{1,3,2,0:T(8,128)(2,1)} copy(bf16[2,512,12,64]{3,2,1,0:T(8,128)(2,1)} %bitcast.142) | data formatting | bytes 3145728 | tf_op jit(solution)/shard_map/while | solution.py:83
  403.2 32.3 %while.10 = (s32[]{:T(128)}, bf16[2,512,12,64]{1,3,2,0:T(8,128)(2,1)S(1)}, bf16[2,512,12,64]{1,3,2,0:T(8,128)(2,1)}, bf16[2,512,12,64]{1,3,2,0:T(8,128)(2,1)}, bf16[2,512,12,64]{1,3,2,0:T(8,128)(2,1)}, /*index=5*/s32[]{:T(128)}) while((s32[]{:T(128)}, bf16[2,512,12,64]{1,3,2,0:T(8,128)(2,1)S(1)}, bf16[2,512,12,64]{1,3,2,0:T(8,128)(2,1)}, ...), condition=%wide.region_10.11_spmd, body=%wide.region_7.10_spmd.sunk | while | flops 821428736 | bytes 28371012 | solution.py:83
  403.2 10.1 %fusion.105 = (f32[12,512]{1,0:T(8,128)S(1)}, f32[12,512,512]{1,2,0:T(8,128)}) fusion(bf16[2,512,12,64]{1,3,2,0:T(8,128)(2,1)} %get-tuple-element.108, s32[]{:T(128)} %get-tuple-element.98, bf16[2,512,12,64]{1,3,2,0:T(8,128)(2,1)} %get-tuple-element.107), kind=kOutput, calls=%fused_computation.82.clone.1 | convolution fusion | flops 412090880 | bytes 14181376 | tf_op jit(solution)/shard_map/while/body/eval_jaxpr/sub | solution.py:78
  413.3 6.0 %fusion.106 = bf16[2,512,12,64]{1,3,2,0:T(8,128)(2,1)S(1)} fusion(bf16[2,512,12,64]{1,3,2,0:T(8,128)(2,1)S(1)} %get-tuple-element.99, s32[]{:T(128)} %get-tuple-element.98, f32[12,512,512]{1,2,0:T(8,128)} %get-tuple-element.90, f32[12,512]{1,0:T(8,128)S(1)} %get-tuple-element.91, bf16[2,512,12,64]{1,3,2,0:T(8,128)(2,1)} %get-tuple-element.106), kind=kOutput, calls=%fused_computation.10.clone.1 | convolution fusion | flops 409337856 | bytes 14189568 | tf_op jit(solution)/shard_map/while/body/eval_jaxpr/hrs,shd->rhd/dot_general | solution.py:79
  419.4 10.1 %fusion.105 = (f32[12,512]{1,0:T(8,128)S(1)}, f32[12,512,512]{1,2,0:T(8,128)}) fusion(bf16[2,512,12,64]{1,3,2,0:T(8,128)(2,1)} %get-tuple-element.108, s32[]{:T(128)} %get-tuple-element.98, bf16[2,512,12,64]{1,3,2,0:T(8,128)(2,1)} %get-tuple-element.107), kind=kOutput, calls=%fused_computation.82.clone.1 | convolution fusion | flops 412090880 | bytes 14181376 | tf_op jit(solution)/shard_map/while/body/eval_jaxpr/sub | solution.py:78
  429.4 6.0 %fusion.106 = bf16[2,512,12,64]{1,3,2,0:T(8,128)(2,1)S(1)} fusion(bf16[2,512,12,64]{1,3,2,0:T(8,128)(2,1)S(1)} %get-tuple-element.99, s32[]{:T(128)} %get-tuple-element.98, f32[12,512,512]{1,2,0:T(8,128)} %get-tuple-element.90, f32[12,512]{1,0:T(8,128)S(1)} %get-tuple-element.91, bf16[2,512,12,64]{1,3,2,0:T(8,128)(2,1)} %get-tuple-element.106), kind=kOutput, calls=%fused_computation.10.clone.1 | convolution fusion | flops 409337856 | bytes 14189568 | tf_op jit(solution)/shard_map/while/body/eval_jaxpr/hrs,shd->rhd/dot_general | solution.py:79
  441.5 26.7 %all_to_all.119 = bf16[512,2,768]{2,1,0:T(2,128)(2,1)S(1)} all-to-all(bf16[512,2,768]{2,1,0:T(2,128)(2,1)S(1)} %copy.55), channel_id=1, replica_groups=mesh['seq'=16,'res'=8] {'seq'}, dimensions={0} | all-to-all | bytes 3145728 | tf_op jit(solution)/shard_map/all_to_all | solution.py:86
  471.6 5.4 %reshape.70 = f32[32,32,768]{2,1,0:T(8,128)} reshape(f32[32,16,2,768]{3,2,1,0:T(2,128)} %copy_bitcast_fusion) | data formatting | bytes 6291456 | tf_op jit(solution)/shard_map/convert_element_type | solution.py:87
  (53 shorter events, 56.1 us)
Async XLA Ops:
  6.5 287.9 %copy-start = (bf16[768,768]{1,0:T(8,128)(2,1)S(1)}, bf16[768,768]{1,0:T(8,128)(2,1)}, u32[]{:S(2)}) copy-start(bf16[768,768]{1,0:T(8,128)(2,1)} %param.15) | copy-start | bytes 3538948
  6.5 2.0 copy-start.2
  6.5 2.6 copy-start.6
  11.7 31.5 %all-to-all-start.1 = ((bf16[32,32,768]{2,1,0:T(8,128)(2,1)}), bf16[32,32,768]{2,1,0:T(8,128)(2,1)}, u32[]{:S(2)}, u32[]{:S(2)}) async-start(bf16[32,32,768]{2,1,0:T(8,128)(2,1)} %convolution_convert_fusion.5), calls=%async_computation.1 | async-start | bytes 3145728 | tf_op jit(solution)/shard_map/all_to_all | solution.py:38
  43.2 26.4 %all-to-all-start.2 = ((bf16[32,32,768]{2,1,0:T(8,128)(2,1)}), bf16[32,32,768]{2,1,0:T(8,128)(2,1)}, u32[]{:S(2)}, u32[]{:S(2)}) async-start(bf16[32,32,768]{2,1,0:T(8,128)(2,1)} %convolution_convert_fusion.4), calls=%async_computation.2 | async-start | bytes 3145728 | tf_op jit(solution)/shard_map/all_to_all | solution.py:39
  47.5 198.0 %all-reduce.2.cloned.1.call-start = ((), (), s32[]{:S(2)}) async-start(), calls=%async_computation.8 | async-start | bytes 6291456 | tf_op jit(solution)/shard_map/psum | solution.py:51
  295.9 3.4 copy-start.3
  296.0 1.8 copy-start.7
  301.3 27.8 %all-to-all-start.6 = ((bf16[32,32,768]{2,0,1:T(8,128)(2,1)}), bf16[32,32,768]{2,0,1:T(8,128)(2,1)S(1)}, u32[]{:S(2)}, u32[]{:S(2)}) async-start(bf16[32,32,768]{2,0,1:T(8,128)(2,1)} %copy.49), calls=%async_computation.6 | async-start | bytes 3145728 | tf_op jit(solution)/shard_map/all_to_all | solution.py:65
  329.1 26.5 %all-to-all-start.5 = ((bf16[32,32,768]{2,0,1:T(8,128)(2,1)}), bf16[32,32,768]{2,0,1:T(8,128)(2,1)}, u32[]{:S(2)}, u32[]{:S(2)}) async-start(bf16[32,32,768]{2,0,1:T(8,128)(2,1)} %copy.47), calls=%async_computation.5 | async-start | bytes 3145728 | tf_op jit(solution)/shard_map/all_to_all | solution.py:64
  355.7 36.7 %all-to-all-start.4 = ((bf16[32,32,768]{2,0,1:T(8,128)(2,1)}), bf16[32,32,768]{2,0,1:T(8,128)(2,1)}, u32[]{:S(2)}, u32[]{:S(2)}) async-start(bf16[32,32,768]{2,0,1:T(8,128)(2,1)} %copy.45), calls=%async_computation.4 | async-start | bytes 3145728 | tf_op jit(solution)/shard_map/all_to_all | solution.py:66
  397.8 5.5 %copy-start.5 = (bf16[2,512,12,64]{1,3,2,0:T(8,128)(2,1)S(1)}, bf16[2,512,12,64]{1,3,2,0:T(8,128)(2,1)}, u32[]{:S(2)}) copy-start(bf16[2,512,12,64]{1,3,2,0:T(8,128)(2,1)} %custom-call) | copy-start | bytes 4718596
  435.5 1.6 copy-start.8
  471.6 5.4 %copy-start.4 = (bf16[32,32,768]{2,1,0:T(8,128)(2,1)S(1)}, bf16[32,32,768]{2,1,0:T(8,128)(2,1)}, u32[]{:S(2)}) copy-start(bf16[32,32,768]{2,1,0:T(8,128)(2,1)} %copy-done.3) | copy-start | bytes 4718596
  477.0 3.6 copy-start.1
Sparse Core Ops, SparseCore 0:
  85.1 160.3 all-reduce.1
where the time goes:
time: 496 us; the launch traced here: 488 us
  waiting for transfers between devices  189 us (38%)
  local copies, waits for them, and re-layouts  81.2 us (16%)
  blocking collectives  79.4 us (16%)
  matrix products  72.8 us (15%)
  starting transfers between devices  37.3 us (8%)
  between operations  13.9 us (3%)
  other arithmetic  13.8 us (3%)
    psum x1, waiting for transfers between devices, on_device(): tied = lax.psum(partial_value, ('seq', 'res'))  124 us
    all_to_all x1, blocking collectives, on_device(): lax.all_to_all(v1, 'res', split_axis=0, concat_axis=1, tiled=True)  26.8 us
    all_to_all x1, blocking collectives, on_device(): lax.all_to_all(colupd, 'seq', split_axis=0, concat_axis=1, tiled=True)  26.7 us
    all_to_all x1, blocking collectives, on_device(): o1 = lax.all_to_all(o_moved, 'res', split_axis=1, concat_axis=0, tiled=True)  25.9 us
    dot_general x8, matrix products, project(): return jnp.dot(inputs, weight, preferred_element_type=jnp.float32)  21.4 us
    sub x2, matrix products, attend(): prob2 = jax.nn.softmax(score, axis=-1).astype(jnp.bfloat16)  20.1 us
    all_to_all x1, waiting for transfers between devices, on_device(): lax.all_to_all(q1, 'res', split_axis=0, concat_axis=1, tiled=True)  19.3 us
    reshape x3, local copies, waits for them, and re-layouts, split_heads(): return field.reshape(field.shape[0], field.shape[1], HEADS, D // HEADS)  17.7 us
  transfers between devices with their start and end apart: 6, of which 5 were waited for; matrix products, arithmetic and copies ran while one was open for 11% of the time, Pallas kernels for 0%

commit v1 on v0

--- a/solution.py
+++ b/solution.py
@@ -48,7 +48,8 @@
         )
         * tied_scale
     )
-    tied = lax.psum(partial_value, ("seq", "res"))
+    partial = lax.psum(partial_value, "seq")
+    tied = lax.psum(partial, "res")
     prob1 = jax.nn.softmax(tied, axis=-1).astype(jnp.bfloat16)
     o_moved = jnp.einsum(
         "hij,rjhd->rihd", prob1, split_heads(v_moved), preferred_element_type=jnp.float32

time: 496 us -> 624 us (1.26)
  waiting for transfers between devices: 189 us -> 310 us
  blocking collectives: 79.4 us -> 86.2 us
    psum x1 -> x2, waiting for transfers between devices: 124 us -> 245 us  [the longest x1 124 us: on_device(): partial = lax.psum(partial_value, 'seq')]
  transfers between devices with their start and end apart: 6 -> 7, of which waited for: 5 -> 6; matrix products, arithmetic and copies ran while one was open for 11% -> 9% of each run, Pallas kernels for 0% -> 0%
where the time goes in v1:
time: 624 us; the launch traced here: 616 us
  waiting for transfers between devices  310 us (50%)
  blocking collectives  86.2 us (14%)
  local copies, waits for them, and re-layouts  81.2 us (13%)
  matrix products  72.8 us (12%)
  starting transfers between devices  38.1 us (6%)
  between operations  13.9 us (2%)
  other arithmetic  13.8 us (2%)
    psum x1, waiting for transfers between devices, on_device(): partial = lax.psum(partial_value, 'seq')  124 us
    psum x1, waiting for transfers between devices, on_device(): tied = lax.psum(partial, 'res')  120 us
    all_to_all x1, blocking collectives, on_device(): lax.all_to_all(v1, 'res', split_axis=0, concat_axis=1, tiled=True)  30.8 us
    all_to_all x1, blocking collectives, on_device(): o1 = lax.all_to_all(o_moved, 'res', split_axis=1, concat_axis=0, tiled=True)  28.7 us
    all_to_all x1, blocking collectives, on_device(): lax.all_to_all(colupd, 'seq', split_axis=0, concat_axis=1, tiled=True)  26.7 us
    dot_general x8, matrix products, project(): return jnp.dot(inputs, weight, preferred_element_type=jnp.float32)  21.4 us
    sub x2, matrix products, attend(): prob2 = jax.nn.softmax(score, axis=-1).astype(jnp.bfloat16)  20.1 us
    all_to_all x1, waiting for transfers between devices, on_device(): lax.all_to_all(q1, 'res', split_axis=0, concat_axis=1, tiled=True)  19.3 us
  transfers between devices with their start and end apart: 7, of which 6 were waited for; matrix products, arithmetic and copies ran while one was open for 9% of the time, Pallas kernels for 0%

profile of v1, /device:TPU:1, one launch (start us, length us, event | category | flops | bytes accessed | tf_op | source)
XLA Modules:
  0.0 616.1 jit_solution(1011375208847591836)
XLA Ops:
  11.7 8.3 %all-to-all-start.1 = ((bf16[32,32,768]{2,1,0:T(8,128)(2,1)}), bf16[32,32,768]{2,1,0:T(8,128)(2,1)}, u32[]{:S(2)}, u32[]{:S(2)}) async-start(bf16[32,32,768]{2,1,0:T(8,128)(2,1)} %convolution_convert_fusion.5), calls=%async_computation.1 | async-start | bytes 3145728 | tf_op jit(solution)/shard_map/all_to_all | solution.py:38
  20.1 3.9 convolution_convert_fusion.4
  23.9 19.3 %all-to-all-done.1 = bf16[32,32,768]{2,1,0:T(8,128)(2,1)} async-done(((bf16[32,32,768]{2,1,0:T(8,128)(2,1)}), bf16[32,32,768]{2,1,0:T(8,128)(2,1)}, u32[]{:S(2)}, u32[]{:S(2)}) %all-to-all-start.1) | async-done | bytes 1572896 | tf_op jit(solution)/shard_map/all_to_all | solution.py:38
  43.2 4.3 all-to-all-start.2
  50.3 5.9 reshape.63
  56.2 13.5 %all-to-all-done.2 = bf16[32,32,768]{2,1,0:T(8,128)(2,1)} async-done(((bf16[32,32,768]{2,1,0:T(8,128)(2,1)}), bf16[32,32,768]{2,1,0:T(8,128)(2,1)}, u32[]{:S(2)}, u32[]{:S(2)}) %all-to-all-start.2) | async-done | bytes 1572896 | tf_op jit(solution)/shard_map/all_to_all | solution.py:39
  72.3 5.9 reshape.64
  78.2 6.7 %bitcast_multiply_fusion = f32[12,256,256]{2,1,0:T(8,128)} fusion(bf16[4,256,12,64]{3,2,1,0:T(8,128)(2,1)} %reshape.64, bf16[4,256,12,64]{3,2,1,0:T(8,128)(2,1)} %reshape.63), kind=kOutput, calls=%fused_computation.43 | convolution fusion | flops 403439616 | bytes 6291456 | tf_op jit(solution)/shard_map/rihd,rjhd->hij/dot_general | solution.py:43
  85.0 124.3 %all-reduce.3.cloned.1.call-done = f32[12,256,256]{2,1,0:T(8,128)} async-done(((f32[12,256,256]{2,1,0:T(8,128)}), f32[12,256,256]{2,1,0:T(8,128)}) %all-reduce.3.cloned.1.call-update) | async-done | bytes 3145744 | tf_op jit(solution)/shard_map/psum | solution.py:51
  212.1 30.8 %all_to_all.117 = bf16[32,32,768]{2,1,0:T(8,128)(2,1)S(1)} all-to-all(bf16[32,32,768]{2,1,0:T(8,128)(2,1)S(1)} %convolution_convert_fusion.6), channel_id=1, replica_groups=mesh['seq'=16,'res'=8] {'res'}, dimensions={0} | all-to-all | bytes 3145728 | tf_op jit(solution)/shard_map/all_to_all | solution.py:40
  244.1 5.9 reshape.62
  250.0 120.3 %all-reduce.5.cloned.1.call-done = f32[12,256,256]{2,1,0:T(8,128)} async-done(((f32[12,256,256]{2,1,0:T(8,128)}), f32[12,256,256]{2,1,0:T(8,128)}) %all-reduce.5.cloned.1.call-update) | async-done | bytes 3145744 | tf_op jit(solution)/shard_map/psum | solution.py:52
  374.0 12.5 %fusion.63 = bf16[4,256,12,64]{1,3,0,2:T(8,128)(2,1)} fusion(f32[12,256]{1,0:T(8,128)S(1)} %fusion.92, bf16[4,256,12,64]{3,2,1,0:T(8,128)(2,1)} %reshape.62, f32[12,256,256]{2,1,0:T(8,128)} %all-reduce.5.cloned.1.call-done), kind=kOutput, calls=%fused_computation.68 | convolution fusion | flops 405802240 | bytes 6303744 | tf_op jit(solution)/shard_map/hij,rjhd->rihd/dot_general | solution.py:54
  393.0 28.7 %all_to_all.118 = bf16[4,256,768]{2,0,1:T(4,128)(2,1)S(1)} all-to-all(bf16[4,256,768]{2,0,1:T(4,128)(2,1)} %copy.42), channel_id=1, replica_groups=mesh['seq'=16,'res'=8] {'res'}, dimensions={1} | all-to-all | bytes 3145728 | tf_op jit(solution)/shard_map/all_to_all | solution.py:58
  428.9 7.1 %all-to-all-start.6 = ((bf16[32,32,768]{2,0,1:T(8,128)(2,1)}), bf16[32,32,768]{2,0,1:T(8,128)(2,1)S(1)}, u32[]{:S(2)}, u32[]{:S(2)}) async-start(bf16[32,32,768]{2,0,1:T(8,128)(2,1)} %copy.49), calls=%async_computation.6 | async-start | bytes 3145728 | tf_op jit(solution)/shard_map/all_to_all | solution.py:66
  441.2 16.3 %all-to-all-done.6 = bf16[32,32,768]{2,0,1:T(8,128)(2,1)S(1)} async-done(((bf16[32,32,768]{2,0,1:T(8,128)(2,1)}), bf16[32,32,768]{2,0,1:T(8,128)(2,1)S(1)}, u32[]{:S(2)}, u32[]{:S(2)}) %all-to-all-start.6) | async-done | bytes 1572896 | tf_op jit(solution)/shard_map/all_to_all | solution.py:66
  457.5 4.9 all-to-all-start.5
  467.6 16.4 %all-to-all-done.5 = bf16[32,32,768]{2,0,1:T(8,128)(2,1)} async-done(((bf16[32,32,768]{2,0,1:T(8,128)(2,1)}), bf16[32,32,768]{2,0,1:T(8,128)(2,1)}, u32[]{:S(2)}, u32[]{:S(2)}) %all-to-all-start.5) | async-done | bytes 1572896 | tf_op jit(solution)/shard_map/all_to_all | solution.py:65
  484.0 13.4 %all-to-all-start.4 = ((bf16[32,32,768]{2,0,1:T(8,128)(2,1)}), bf16[32,32,768]{2,0,1:T(8,128)(2,1)}, u32[]{:S(2)}, u32[]{:S(2)}) async-start(bf16[32,32,768]{2,0,1:T(8,128)(2,1)} %copy.45), calls=%async_computation.4 | async-start | bytes 3145728 | tf_op jit(solution)/shard_map/all_to_all | solution.py:67
  498.8 5.9 reshape.68
  504.6 5.3 copy.53
  511.5 3.9 reshape.67
  515.4 5.3 copy.52
  522.2 3.9 reshape.66
  526.1 5.5 copy.51
  531.5 32.3 %while.10 = (s32[]{:T(128)}, bf16[2,512,12,64]{1,3,2,0:T(8,128)(2,1)S(1)}, bf16[2,512,12,64]{1,3,2,0:T(8,128)(2,1)}, bf16[2,512,12,64]{1,3,2,0:T(8,128)(2,1)}, bf16[2,512,12,64]{1,3,2,0:T(8,128)(2,1)}, /*index=5*/s32[]{:T(128)}) while((s32[]{:T(128)}, bf16[2,512,12,64]{1,3,2,0:T(8,128)(2,1)S(1)}, bf16[2,512,12,64]{1,3,2,0:T(8,128)(2,1)}, ...), condition=%wide.region_11.12_spmd, body=%wide.region_8.11_spmd.sunk | while | flops 821428736 | bytes 28371012 | solution.py:84
  531.5 10.1 %fusion.105 = (f32[12,512]{1,0:T(8,128)S(1)}, f32[12,512,512]{1,2,0:T(8,128)}) fusion(bf16[2,512,12,64]{1,3,2,0:T(8,128)(2,1)} %get-tuple-element.108, s32[]{:T(128)} %get-tuple-element.98, bf16[2,512,12,64]{1,3,2,0:T(8,128)(2,1)} %get-tuple-element.107), kind=kOutput, calls=%fused_computation.82.clone.1 | convolution fusion | flops 412090880 | bytes 14181376 | tf_op jit(solution)/shard_map/while/body/eval_jaxpr/sub | solution.py:79
  541.6 6.0 fusion.106
  547.7 10.1 %fusion.105 = (f32[12,512]{1,0:T(8,128)S(1)}, f32[12,512,512]{1,2,0:T(8,128)}) fusion(bf16[2,512,12,64]{1,3,2,0:T(8,128)(2,1)} %get-tuple-element.108, s32[]{:T(128)} %get-tuple-element.98, bf16[2,512,12,64]{1,3,2,0:T(8,128)(2,1)} %get-tuple-element.107), kind=kOutput, calls=%fused_computation.82.clone.1 | convolution fusion | flops 412090880 | bytes 14181376 | tf_op jit(solution)/shard_map/while/body/eval_jaxpr/sub | solution.py:79
  557.8 6.0 fusion.106
  569.8 26.7 %all_to_all.119 = bf16[512,2,768]{2,1,0:T(2,128)(2,1)S(1)} all-to-all(bf16[512,2,768]{2,1,0:T(2,128)(2,1)S(1)} %copy.55), channel_id=1, replica_groups=mesh['seq'=16,'res'=8] {'seq'}, dimensions={0} | all-to-all | bytes 3145728 | tf_op jit(solution)/shard_map/all_to_all | solution.py:87
  600.0 5.4 reshape.70
  (56 shorter events, 59.9 us)
Async XLA Ops:
  6.5 415.5 %copy-start = (bf16[768,768]{1,0:T(8,128)(2,1)S(1)}, bf16[768,768]{1,0:T(8,128)(2,1)}, u32[]{:S(2)}) copy-start(bf16[768,768]{1,0:T(8,128)(2,1)} %param.15) | copy-start | bytes 3538948
  6.5 2.0 copy-start.2
  6.5 2.6 copy-start.6
  11.7 31.5 %all-to-all-start.1 = ((bf16[32,32,768]{2,1,0:T(8,128)(2,1)}), bf16[32,32,768]{2,1,0:T(8,128)(2,1)}, u32[]{:S(2)}, u32[]{:S(2)}) async-start(bf16[32,32,768]{2,1,0:T(8,128)(2,1)} %convolution_convert_fusion.5), calls=%async_computation.1 | async-start | bytes 3145728 | tf_op jit(solution)/shard_map/all_to_all | solution.py:38
  43.2 26.4 %all-to-all-start.2 = ((bf16[32,32,768]{2,1,0:T(8,128)(2,1)}), bf16[32,32,768]{2,1,0:T(8,128)(2,1)}, u32[]{:S(2)}, u32[]{:S(2)}) async-start(bf16[32,32,768]{2,1,0:T(8,128)(2,1)} %convolution_convert_fusion.4), calls=%async_computation.2 | async-start | bytes 3145728 | tf_op jit(solution)/shard_map/all_to_all | solution.py:39
  47.5 161.8 %all-reduce.3.cloned.1.call-start = ((), (), s32[]{:S(2)}) async-start(), calls=%async_computation.8 | async-start | bytes 6291456 | tf_op jit(solution)/shard_map/psum | solution.py:51
  85.0 285.3 %all-reduce.5.cloned.1.call-start = ((), (), s32[]{:S(2)}) async-start(), calls=%async_computation.9 | async-start | bytes 6291456 | tf_op jit(solution)/shard_map/psum | solution.py:52
  423.5 3.3 copy-start.3
  423.5 1.8 copy-start.7
  428.9 28.6 %all-to-all-start.6 = ((bf16[32,32,768]{2,0,1:T(8,128)(2,1)}), bf16[32,32,768]{2,0,1:T(8,128)(2,1)S(1)}, u32[]{:S(2)}, u32[]{:S(2)}) async-start(bf16[32,32,768]{2,0,1:T(8,128)(2,1)} %copy.49), calls=%async_computation.6 | async-start | bytes 3145728 | tf_op jit(solution)/shard_map/all_to_all | solution.py:66
  457.5 26.5 %all-to-all-start.5 = ((bf16[32,32,768]{2,0,1:T(8,128)(2,1)}), bf16[32,32,768]{2,0,1:T(8,128)(2,1)}, u32[]{:S(2)}, u32[]{:S(2)}) async-start(bf16[32,32,768]{2,0,1:T(8,128)(2,1)} %copy.47), calls=%async_computation.5 | async-start | bytes 3145728 | tf_op jit(solution)/shard_map/all_to_all | solution.py:65
  484.0 36.7 %all-to-all-start.4 = ((bf16[32,32,768]{2,0,1:T(8,128)(2,1)}), bf16[32,32,768]{2,0,1:T(8,128)(2,1)}, u32[]{:S(2)}, u32[]{:S(2)}) async-start(bf16[32,32,768]{2,0,1:T(8,128)(2,1)} %copy.45), calls=%async_computation.4 | async-start | bytes 3145728 | tf_op jit(solution)/shard_map/all_to_all | solution.py:67
  526.1 5.5 copy-start.5
  563.8 1.6 copy-start.8
  600.0 5.4 copy-start.4
  605.4 3.6 copy-start.1
Sparse Core Ops, SparseCore 0:
  85.1 124.1 all-reduce.2
  211.8 158.4 all-reduce.4
